TPU v7x, 128 devices: a whole 4x4x4 slice. The times are simulated.
128 devices in a mesh: sub: 32 (over x, y, core), rep: 4 (over z).
Axes of the slice: x: 4, y: 4, z: 4, core: 2. Of those that a mesh axis runs over, the one named last changes fastest.
Arguments:
- loads: bfloat16 [256, 256, 1024], P('sub', 'rep'), may hold values from -6 to 6
- operators: bfloat16 [256, 1024, 1024], P('sub'), may hold values from -0.1875 to 0.1875
- owner: int32 [2048, 1], P('sub'), may hold values from 0 to 31; in each aligned block of 64 rows (0 to 63, 64 to 127, ...) at most 4 rows name the same one
- dual_block: int32 [2048], P('sub'), may hold values from 0 to 15
- scale_index: int32 [65536], P('sub'), may hold values from 0 to 3
- basis: bfloat16 [65536, 1024], P('sub'), may hold values from -0.0234375 to 0.0234375
- coarse: bfloat16 [1024, 1024], replicated, may hold values from -1.5 to 1.5
Outputs:
- start: float32 [256, 65536], P('rep', 'sub')
- resid: float32 [256, 65536], P('rep', 'sub')
Inputs may be any that keep to these rules, and one draw needn't show every extreme that they name: Among the blocks of the subdomains of one index of sub (aligned blocks of 64 rows), no owner is named more than 4 times, a bound that some block reaches.
All inputs are finite; a program needn't handle non-finite values.
Results may differ from a plain program's by a relative error of at most 0.0075.
Values may be sent and summed in bfloat16 or wider, within the bound.
No kernel may reach another device: no remote copies, remote signals or barrier semaphores. Data moves between devices by JAX's collectives and lax.ppermute only.
A program may use at most 128 MiB of HBM per device.

v0:
```python
import jax
import jax.numpy as jnp
from jax import lax
from jax.sharding import PartitionSpec as P

BLK = 128


def apply_local(inputs, operators):
    return jnp.einsum("skl,slm->skm", inputs, operators, preferred_element_type=jnp.float32).astype(
        jnp.bfloat16
    )


def make_blocks(values, width):
    count, columns, local = values.shape
    return (
        values.reshape(count, columns, local // width, width)
        .transpose(0, 2, 1, 3)
        .reshape(-1, columns, width)
    )


def from_blocks(blocks, count):
    total, columns, width = blocks.shape
    per_sub = total // count
    return (
        blocks.reshape(count, per_sub, columns, width)
        .transpose(0, 2, 1, 3)
        .reshape(count, columns, per_sub * width)
    )


def pack_slots(blocks, dests, ranks, peers, slots):
    columns, width = (blocks.shape[1], blocks.shape[2])
    return jnp.zeros((peers, slots, columns, width), jnp.bfloat16).at[dests, ranks].set(blocks)


def accumulate(received, got_ids, own_blocks, weight):
    columns, width = (received.shape[2], received.shape[3])
    flat = received.reshape(-1, columns, width).astype(jnp.float32)
    total = jnp.zeros((own_blocks, columns, width), jnp.float32).at[got_ids.reshape(-1)].add(flat)
    return total.transpose(1, 0, 2).reshape(columns, own_blocks * width) * weight[None, :]


def per_device(loads, operators, owner, dual_block, scale_index, basis, coarse):
    sub_count = loads.shape[0]
    width = BLK
    peers = lax.axis_size("sub")
    dests = owner[:, 0]
    nblocks = dests.shape[0]
    slots = max(2, 2 * nblocks // peers)
    own_blocks = basis.shape[0] // width
    positions = jnp.arange(nblocks, dtype=jnp.int32)
    earlier = positions[None, :] < positions[:, None]
    same = dests[None, :] == dests[:, None]
    ranks = jnp.sum(jnp.logical_and(earlier, same), axis=1)
    weight = 1.0 / (1.0 + scale_index.astype(jnp.float32))
    terms = apply_local(loads, operators)
    packed = pack_slots(make_blocks(terms, width), dests, ranks, peers, slots)
    id_slots = jnp.zeros((peers, slots), jnp.int32).at[dests, ranks].set(dual_block)
    received, got_ids = (
        lax.all_to_all(packed, "sub", split_axis=0, concat_axis=0, tiled=True),
        lax.all_to_all(id_slots, "sub", split_axis=0, concat_axis=0, tiled=True),
    )
    dual = accumulate(received, got_ids, own_blocks, weight)
    coeff = jnp.dot(dual.astype(jnp.bfloat16), basis, preferred_element_type=jnp.float32)
    summed = lax.psum(coeff, "sub")
    solved = jnp.dot(
        summed.astype(jnp.bfloat16), coarse, preferred_element_type=jnp.float32
    ).astype(jnp.bfloat16)
    start = lax.dot_general(
        solved, basis, (((1,), (1,)), ((), ())), preferred_element_type=jnp.float32
    )
    columns = start.shape[0]
    start_blocks = start.astype(jnp.bfloat16).reshape(columns, own_blocks, width).transpose(1, 0, 2)
    requested = start_blocks[got_ids]
    returned = lax.all_to_all(requested, "sub", split_axis=0, concat_axis=0, tiled=True)
    picked = returned[dests, ranks]
    local = from_blocks(picked, sub_count)
    again = apply_local(local, operators)
    received_again = lax.all_to_all(
        pack_slots(make_blocks(again, width), dests, ranks, peers, slots),
        "sub",
        split_axis=0,
        concat_axis=0,
        tiled=True,
    )
    applied = accumulate(received_again, got_ids, own_blocks, weight)
    return (start, dual - applied)


def solution(mesh):
    return jax.shard_map(
        per_device,
        mesh=mesh,
        in_specs=(
            P("sub", "rep", None),
            P("sub", None, None),
            P("sub", None),
            P("sub"),
            P("sub"),
            P("sub", None),
            P(),
        ),
        out_specs=(P("rep", "sub"), P("rep", "sub")),
        check_vma=False,
    )
```

profile of v0, /device:TPU:1, one launch (start us, length us, event | category | flops | bytes accessed | tf_op | source)
XLA Modules:
  0.0 336.0 jit_solution(8166071477639882503)
XLA Ops:
  0.6 0.0 copy-start
  0.6 1.0 convert_reduce_fusion
  1.6 0.7 fusion.15
  2.3 5.7 %scatter_fusion = s32[32,4]{0,1:T(4,128)S(1)} fusion(s32[32,4]{0,1:T(4,128)S(1)} %broadcast.75, s32[64]{0:T(128)S(1)} %get-tuple-element.2, s32[64]{0:T(128)} %param.10), kind=kCustom, calls=%fused_computation.2 | custom fusion | bytes 1280 | tf_op jit(solution)/shard_map/scatter | solution.py:61
  8.1 0.7 copy.33
  8.8 8.6 %all-to-all-start = ((s32[32,1,4]{2,1,0:T(1,128)}), s32[32,1,4]{2,1,0:T(1,128)S(1)}, u32[]{:S(2)}, u32[]{:S(2)}) async-start(s32[32,1,4]{2,1,0:T(1,128)} %copy.33), calls=%async_computation | async-start | bytes 32768 | tf_op jit(solution)/shard_map/all_to_all | solution.py:64
  17.4 9.1 %fusion = bf16[8,8,8,8,128]{4,3,2,1,0:T(8,128)(2,1)S(1)} fusion(bf16[8,64,1024]{2,1,0:T(8,128)(2,1)} %param.7, bf16[8,1024,1024]{2,1,0:T(8,128)(2,1)} %param.8), kind=kOutput, calls=%fused_computation.11 | convolution fusion | flops 1074266112 | bytes 18874368 | tf_op jit(solution)/shard_map/skl,slm->skm/dot_general | solution.py:10
  26.5 0.3 copy.63
  26.8 1.9 broadcast.81.clone
  28.7 8.9 %scatter_fusion.1 = bf16[32,4,64,128]{3,2,1,0:T(8,128)(2,1)} fusion(bf16[32,4,64,128]{3,2,1,0:T(8,128)(2,1)} %broadcast.81.clone, s32[64]{0:T(128)S(1)} %get-tuple-element.2, bf16[64,64,128]{2,1,0:T(8,128)(2,1)S(1)} %bitcast.87), kind=kCustom, calls=%fused_computation.3 | custom fusion | bytes 3146240 | tf_op jit(solution)/shard_map/scatter | solution.py:36
  37.5 0.0 copy-start.1
  37.5 0.0 all-to-all-done
  37.5 7.6 %all-to-all-start.1 = ((bf16[32,4,64,128]{3,2,1,0:T(8,128)(2,1)}), bf16[32,4,64,128]{3,2,1,0:T(8,128)(2,1)}, u32[]{:S(2)}, u32[]{:S(2)}) async-start(bf16[32,4,64,128]{3,2,1,0:T(8,128)(2,1)} %scatter_fusion.1), calls=%async_computation.1 | async-start | bytes 4194304 | tf_op jit(solution)/shard_map/all_to_all | solution.py:63
  45.1 0.0 copy-done.1
  45.1 0.5 broadcast.184
  45.7 0.7 reduce.3
  46.4 0.1 reshape.115
  46.5 0.1 copy.37
  46.5 0.1 copy.38
  46.6 0.1 reshape.129
  46.8 26.7 %all-to-all-done.1 = bf16[32,4,64,128]{3,2,1,0:T(8,128)(2,1)} async-done(((bf16[32,4,64,128]{3,2,1,0:T(8,128)(2,1)}), bf16[32,4,64,128]{3,2,1,0:T(8,128)(2,1)}, u32[]{:S(2)}, u32[]{:S(2)}) %all-to-all-start.1) | async-done | bytes 2097184 | tf_op jit(solution)/shard_map/all_to_all | solution.py:63
  73.5 4.0 %bitcast_convert_fusion.1 = f32[128,64,128]{2,1,0:T(8,128)} fusion(bf16[32,4,64,128]{3,2,1,0:T(8,128)(2,1)} %all-to-all-done.1), kind=kLoop, calls=%fused_computation.8 | loop fusion | flops 1048576 | bytes 6291456 | tf_op jit(solution)/shard_map/convert_element_type | solution.py:41
  77.5 13.5 %scatter_fusion.2 = f32[16,64,128]{2,1,0:T(8,128)S(1)} fusion(f32[16,64,128]{2,1,0:T(8,128)S(1)} %broadcast.74.clone, s32[128]{0:T(128)S(1)} %fusion.14, f32[128,64,128]{2,1,0:T(8,128)} %bitcast_convert_fusion.1), kind=kCustom, calls=%fused_computation.4 | custom fusion | flops 1048576 | bytes 12583424 | tf_op jit(solution)/shard_map/scatter-add | solution.py:42
  91.1 3.0 fusion.7
  94.1 121.1 %all-reduce.1 = bf16[64,1024]{1,0:T(8,128)(2,1)S(1)} all-reduce(f32[64,1024]{1,0:T(8,128)S(1)} %fusion.7), channel_id=1, replica_groups=mesh['sub'=32,'rep'=4] {'sub'}, use_global_device_ids=true, to_apply=%region_4.0 | all-reduce | flops 65536 | bytes 393216 | tf_op jit(solution)/shard_map/psum | solution.py:68
  215.3 0.0 copy-done
  215.3 4.8 %fusion.2 = f32[64,2048]{1,0:T(8,128)} fusion(bf16[2048,1024]{1,0:T(8,128)(2,1)} %param.12, bf16[1024,1024]{1,0:T(8,128)(2,1)S(1)} %copy-done, bf16[64,1024]{1,0:T(8,128)(2,1)S(1)} %all-reduce.1), kind=kOutput, calls=%fused_computation.14 | convolution fusion | flops 402718720 | bytes 6946816 | tf_op jit(solution)/shard_map/dot_general | solution.py:72
  220.0 1.1 bitcast_bitcast_fusion
  221.1 2.1 gather_fusion
  223.2 38.3 %all_to_all.27 = bf16[32,4,64,128]{3,2,1,0:T(8,128)(2,1)} all-to-all(bf16[32,4,64,128]{3,2,1,0:T(8,128)(2,1)} %bitcast.85), channel_id=1, replica_groups=mesh['sub'=32,'rep'=4] {'sub'}, dimensions={0} | all-to-all | bytes 4194304 | tf_op jit(solution)/shard_map/all_to_all | solution.py:78
  261.5 3.3 gather_fusion.1
  264.8 9.1 %fusion.1 = bf16[8,8,8,8,128]{4,3,2,1,0:T(8,128)(2,1)S(1)} fusion(bf16[8,1024,1024]{2,1,0:T(8,128)(2,1)} %param.8, bf16[8,8,8,8,128]{4,3,2,1,0:T(8,128)(2,1)} %bitcast.88), kind=kOutput, calls=%fused_computation.12 | convolution fusion | flops 1074266112 | bytes 18874368 | tf_op jit(solution)/shard_map/skl,slm->skm/dot_general | solution.py:10
  273.9 1.3 copy.62
  275.2 1.9 broadcast.81
  277.1 9.8 %scatter_fusion.3 = bf16[32,4,64,128]{3,2,1,0:T(8,128)(2,1)} fusion(bf16[32,4,64,128]{3,2,1,0:T(8,128)(2,1)} %broadcast.81, s32[64]{0:T(128)S(1)} %get-tuple-element.2, bf16[64,64,128]{2,1,0:T(8,128)(2,1)} %bitcast.86), kind=kCustom, calls=%fused_computation.5 | custom fusion | bytes 3146240 | tf_op jit(solution)/shard_map/scatter | solution.py:36
  286.9 32.1 %all_to_all.28 = bf16[32,4,64,128]{3,2,1,0:T(8,128)(2,1)S(1)} all-to-all(bf16[32,4,64,128]{3,2,1,0:T(8,128)(2,1)} %scatter_fusion.3), channel_id=1, replica_groups=mesh['sub'=32,'rep'=4] {'sub'}, dimensions={0} | all-to-all | bytes 4194304 | tf_op jit(solution)/shard_map/all_to_all | solution.py:82
  319.0 2.5 bitcast_convert_fusion
  321.6 13.5 %scatter_fusion.4 = f32[16,64,128]{2,1,0:T(8,128)S(1)} fusion(f32[16,64,128]{2,1,0:T(8,128)S(1)} %broadcast.74, s32[128]{0:T(128)S(1)} %fusion.14, f32[128,64,128]{2,1,0:T(8,128)} %bitcast_convert_fusion), kind=kCustom, calls=%fused_computation.6 | custom fusion | flops 1048576 | bytes 12583424 | tf_op jit(solution)/shard_map/scatter-add | solution.py:42
  335.1 0.9 fusion.5
  (7 shorter events, 0.1 us)
Async XLA Ops:
  0.6 214.6 %copy-start = (bf16[1024,1024]{1,0:T(8,128)(2,1)S(1)}, bf16[1024,1024]{1,0:T(8,128)(2,1)}, u32[]{:S(2)}) copy-start(bf16[1024,1024]{1,0:T(8,128)(2,1)} %param.13) | copy-start | bytes 6291460
  8.8 28.8 %all-to-all-start = ((s32[32,1,4]{2,1,0:T(1,128)}), s32[32,1,4]{2,1,0:T(1,128)S(1)}, u32[]{:S(2)}, u32[]{:S(2)}) async-start(s32[32,1,4]{2,1,0:T(1,128)} %copy.33), calls=%async_computation | async-start | bytes 32768 | tf_op jit(solution)/shard_map/all_to_all | solution.py:64
  37.5 7.6 %copy-start.1 = (s32[2048]{0:T(1024)S(1)}, s32[2048]{0:T(1024)}, u32[]{:S(2)}) copy-start(s32[2048]{0:T(1024)} %param.11) | copy-start | bytes 24580
  37.5 35.9 %all-to-all-start.1 = ((bf16[32,4,64,128]{3,2,1,0:T(8,128)(2,1)}), bf16[32,4,64,128]{3,2,1,0:T(8,128)(2,1)}, u32[]{:S(2)}, u32[]{:S(2)}) async-start(bf16[32,4,64,128]{3,2,1,0:T(8,128)(2,1)} %scatter_fusion.1), calls=%async_computation.1 | async-start | bytes 4194304 | tf_op jit(solution)/shard_map/all_to_all | solution.py:63
where the time goes:
time: 338 us; the launch traced here: 336 us
  blocking collectives  192 us (57%)
  other arithmetic  37.9 us (11%)
  local copies, waits for them, and re-layouts  36.8 us (11%)
  waiting for transfers between devices  26.7 us (8%)
  matrix products  26.1 us (8%)
  starting transfers between devices  16.2 us (5%)
    psum x1, blocking collectives, per_device(): summed = lax.psum(coeff, 'sub')  121 us
    all_to_all x1, blocking collectives, per_device(): lax.all_to_all(requested, 'sub', split_axis=0, concat_axis=0, tiled=True)  38.3 us
    all_to_all x1, blocking collectives, per_device(): lax.all_to_all(pack_slots(make_blocks(again, width), dests, ranks, peers,...  32.1 us
    scatter-add x2, other arithmetic, accumulate(): jnp.zeros((own_blocks, columns, width), jnp.float32).at[got_ids.reshape(-1)]  27.1 us
    all_to_all x1, waiting for transfers between devices, per_device(): lax.all_to_all(packed, 'sub', split_axis=0, concat_axis=0, tiled=True)  26.7 us
    scatter x2, local copies, waits for them, and re-layouts, pack_slots(): jnp.zeros((peers, slots, columns, width), jnp.bfloat16).at[dests, ranks]  18.7 us
    dot_general x2, matrix products, apply_local(): jnp.einsum('skl,slm->skm', inputs, operators, preferred_element_type=jnp....  18.3 us
    all_to_all x1, starting transfers between devices, per_device(): lax.all_to_all(id_slots, 'sub', split_axis=0, concat_axis=0, tiled=True)  8.59 us
  transfers between devices with their start and end apart: 2, of which 1 were waited for; matrix products, arithmetic and copies ran while one was open for 6% of the time, Pallas kernels for 0%

commit v1 on v0

--- a/solution.py
+++ b/solution.py
@@ -4,6 +4,15 @@
 from jax.sharding import PartitionSpec as P
 
 BLK = 128
+
+
+def add_in_pairs(value, mesh_axis):
+    size = lax.axis_size(mesh_axis)
+    acc, far = (value, 1)
+    while far < size:
+        acc = acc + lax.ppermute(acc, mesh_axis, [(i, i ^ far) for i in range(size)])
+        far = 2 * far
+    return acc
 
 
 def apply_local(inputs, operators):
@@ -65,7 +74,7 @@
     )
     dual = accumulate(received, got_ids, own_blocks, weight)
     coeff = jnp.dot(dual.astype(jnp.bfloat16), basis, preferred_element_type=jnp.float32)
-    summed = lax.psum(coeff, "sub")
+    summed = add_in_pairs(coeff, "sub")
     solved = jnp.dot(
         summed.astype(jnp.bfloat16), coarse, preferred_element_type=jnp.float32
     ).astype(jnp.bfloat16)

time: 338 us -> 246 us (0.73)
  blocking collectives: 192 us -> 69.4 us
  waiting for transfers between devices: 26.7 us -> 54.2 us
    psum x1 -> x0, blocking collectives: 121 us -> none  [per_device(): summed = lax.psum(coeff, 'sub')]
    ppermute x0 -> x5, waiting for transfers between devices: none -> 27.2 us  [add_in_pairs(): lax.ppermute(acc, mesh_axis, [(i, i ^ far) for i in range(size)])]
  transfers between devices with their start and end apart: 2 -> 7, of which waited for: 1 -> 6; matrix products, arithmetic and copies ran while one was open for 6% -> 10% of each run, Pallas kernels for 0% -> 0%
where the time goes in v1:
time: 246 us; the launch traced here: 245 us
  blocking collectives  69.4 us (28%)
  waiting for transfers between devices  54.2 us (22%)
  local copies, waits for them, and re-layouts  38.8 us (16%)
  other arithmetic  37 us (15%)
  matrix products  25.3 us (10%)
  starting transfers between devices  19.2 us (8%)
    all_to_all x1, blocking collectives, per_device(): lax.all_to_all(requested, 'sub', split_axis=0, concat_axis=0, tiled=True)  37.3 us
    all_to_all x1, blocking collectives, per_device(): lax.all_to_all(pack_slots(make_blocks(again, width), dests, ranks, peers,...  32.1 us
    ppermute x5, waiting for transfers between devices, add_in_pairs(): lax.ppermute(acc, mesh_axis, [(i, i ^ far) for i in range(size)])  27.2 us
    scatter-add x2, other arithmetic, accumulate(): jnp.zeros((own_blocks, columns, width), jnp.float32).at[got_ids.reshape(-1)]  27.1 us
    all_to_all x1, waiting for transfers between devices, per_device(): lax.all_to_all(packed, 'sub', split_axis=0, concat_axis=0, tiled=True)  27 us
    scatter x2, local copies, waits for them, and re-layouts, pack_slots(): jnp.zeros((peers, slots, columns, width), jnp.bfloat16).at[dests, ranks]  19.6 us
    dot_general x2, matrix products, apply_local(): jnp.einsum('skl,slm->skm', inputs, operators, preferred_element_type=jnp....  18.3 us
    all_to_all x1, starting transfers between devices, per_device(): lax.all_to_all(id_slots, 'sub', split_axis=0, concat_axis=0, tiled=True)  8.59 us
  transfers between devices with their start and end apart: 7, of which 6 were waited for; matrix products, arithmetic and copies ran while one was open for 10% of the time, Pallas kernels for 0%

profile of v1, /device:TPU:1, one launch (start us, length us, event | category | flops | bytes accessed | tf_op | source)
XLA Modules:
  0.0 244.7 jit_solution(18135359633866559109)
XLA Ops:
  0.6 0.0 copy-start
  0.6 1.0 convert_reduce_fusion
  1.6 0.7 fusion.13
  2.3 5.7 %scatter_fusion = s32[32,4]{0,1:T(4,128)S(1)} fusion(s32[32,4]{0,1:T(4,128)S(1)} %broadcast.75, s32[64]{0:T(128)S(1)} %get-tuple-element.2, s32[64]{0:T(128)} %param.10), kind=kCustom, calls=%fused_computation.2 | custom fusion | bytes 1280 | tf_op jit(solution)/shard_map/scatter | solution.py:70
  8.1 0.7 copy.33
  8.8 8.6 %all-to-all-start = ((s32[32,1,4]{2,1,0:T(1,128)}), s32[32,1,4]{2,1,0:T(1,128)S(1)}, u32[]{:S(2)}, u32[]{:S(2)}) async-start(s32[32,1,4]{2,1,0:T(1,128)} %copy.33), calls=%async_computation | async-start | bytes 32768 | tf_op jit(solution)/shard_map/all_to_all | solution.py:73
  17.4 9.1 %fusion = bf16[8,8,8,8,128]{4,3,2,1,0:T(8,128)(2,1)S(1)} fusion(bf16[8,64,1024]{2,1,0:T(8,128)(2,1)} %param.7, bf16[8,1024,1024]{2,1,0:T(8,128)(2,1)} %param.8), kind=kOutput, calls=%fused_computation.11 | convolution fusion | flops 1074266112 | bytes 18874368 | tf_op jit(solution)/shard_map/skl,slm->skm/dot_general | solution.py:19
  26.5 1.3 copy.63
  27.8 1.9 broadcast.81.clone
  29.6 9.8 %scatter_fusion.1 = bf16[32,4,64,128]{3,2,1,0:T(8,128)(2,1)} fusion(bf16[32,4,64,128]{3,2,1,0:T(8,128)(2,1)} %broadcast.81.clone, s32[64]{0:T(128)S(1)} %get-tuple-element.2, bf16[64,64,128]{2,1,0:T(8,128)(2,1)} %bitcast.86), kind=kCustom, calls=%fused_computation.3 | custom fusion | bytes 3146240 | tf_op jit(solution)/shard_map/scatter | solution.py:45
  39.5 0.0 all-to-all-done
  39.5 7.6 %all-to-all-start.1 = ((bf16[32,4,64,128]{3,2,1,0:T(8,128)(2,1)}), bf16[32,4,64,128]{3,2,1,0:T(8,128)(2,1)}, u32[]{:S(2)}, u32[]{:S(2)}) async-start(bf16[32,4,64,128]{3,2,1,0:T(8,128)(2,1)} %scatter_fusion.1), calls=%async_computation.1 | async-start | bytes 4194304 | tf_op jit(solution)/shard_map/all_to_all | solution.py:72
  47.1 0.0 copy-done.2
  47.1 0.5 broadcast.184
  47.6 0.7 reduce.3
  48.3 0.1 reshape.115
  48.4 27.0 %all-to-all-done.1 = bf16[32,4,64,128]{3,2,1,0:T(8,128)(2,1)} async-done(((bf16[32,4,64,128]{3,2,1,0:T(8,128)(2,1)}), bf16[32,4,64,128]{3,2,1,0:T(8,128)(2,1)}, u32[]{:S(2)}, u32[]{:S(2)}) %all-to-all-start.1) | async-done | bytes 2097184 | tf_op jit(solution)/shard_map/all_to_all | solution.py:72
  75.4 4.0 %bitcast_convert_fusion.1 = f32[128,64,128]{2,1,0:T(8,128)} fusion(bf16[32,4,64,128]{3,2,1,0:T(8,128)(2,1)} %all-to-all-done.1), kind=kLoop, calls=%fused_computation.8 | loop fusion | flops 1048576 | bytes 6291456 | tf_op jit(solution)/shard_map/convert_element_type | solution.py:50
  79.4 13.5 %scatter_fusion.2 = f32[16,64,128]{2,1,0:T(8,128)S(1)} fusion(f32[16,64,128]{2,1,0:T(8,128)S(1)} %broadcast.74.clone, s32[128]{0:T(128)S(1)} %fusion.12, f32[128,64,128]{2,1,0:T(8,128)} %bitcast_convert_fusion.1), kind=kCustom, calls=%fused_computation.4 | custom fusion | flops 1048576 | bytes 12583424 | tf_op jit(solution)/shard_map/scatter-add | solution.py:51
  93.0 3.0 %fusion.7 = f32[64,1024]{1,0:T(8,128)S(1)} fusion(bf16[2048,1024]{1,0:T(8,128)(2,1)} %param.12, f32[2048]{0:T(1024)S(1)} %add_divide_fusion, f32[16,64,128]{2,1,0:T(8,128)S(1)} %scatter_fusion.2), kind=kOutput, calls=%fused_computation.23 | convolution fusion | flops 268697600 | bytes 4988928 | tf_op jit(solution)/shard_map/dot_general | solution.py:76
  96.0 0.9 collective-permute-start
  97.0 1.2 collective-permute-done
  98.2 0.1 collective-permute-start.1
  98.3 7.5 %collective-permute-done.1 = f32[64,1024]{1,0:T(8,128)S(1)} collective-permute-done((f32[64,1024]{1,0:T(8,128)S(1)}, f32[64,1024]{1,0:T(8,128)S(1)}, u32[]{:S(2)}, u32[]{:S(2)}) %collective-permute-start.1) | collective-permute-done | bytes 262176 | tf_op jit(solution)/shard_map/ppermute | solution.py:13
  105.8 0.7 collective-permute-start.2
  106.5 7.5 %collective-permute-done.2 = f32[64,1024]{1,0:T(8,128)S(1)} collective-permute-done((f32[64,1024]{1,0:T(8,128)S(1)}, f32[64,1024]{1,0:T(8,128)S(1)}, u32[]{:S(2)}, u32[]{:S(2)}) %collective-permute-start.2) | collective-permute-done | bytes 262176 | tf_op jit(solution)/shard_map/ppermute | solution.py:13
  114.0 0.1 collective-permute-start.3
  114.1 0.1 copy.37
  114.2 5.6 %collective-permute-done.3 = f32[64,1024]{1,0:T(8,128)S(1)} collective-permute-done((f32[64,1024]{1,0:T(8,128)S(1)}, f32[64,1024]{1,0:T(8,128)S(1)}, u32[]{:S(2)}, u32[]{:S(2)}) %collective-permute-start.3) | collective-permute-done | bytes 262176 | tf_op jit(solution)/shard_map/ppermute | solution.py:13
  119.8 1.2 collective-permute-start.4
  121.0 0.1 copy.38
  121.1 0.1 reshape.129
  121.2 5.5 %collective-permute-done.4 = f32[64,1024]{1,0:T(8,128)} collective-permute-done((f32[64,1024]{1,0:T(8,128)S(1)}, f32[64,1024]{1,0:T(8,128)}, u32[]{:S(2)}, u32[]{:S(2)}) %collective-permute-start.4) | collective-permute-done | bytes 262176 | tf_op jit(solution)/shard_map/ppermute | solution.py:13
  126.7 0.0 copy-done
  126.7 4.1 %fusion.2 = f32[64,2048]{1,0:T(8,128)S(1)} fusion(bf16[2048,1024]{1,0:T(8,128)(2,1)} %param.12, bf16[1024,1024]{1,0:T(8,128)(2,1)S(1)} %copy-done, f32[64,1024]{1,0:T(8,128)S(1)} %add.73, f32[64,1024]{1,0:T(8,128)} %collective-permute-done.4), kind=kOutput, calls=%fused_computation.14 | convolution fusion | flops 402849792 | bytes 7340032 | tf_op jit(solution)/shard_map/dot_general | solution.py:81
  130.8 0.0 copy-start.1
  130.9 2.1 gather_fusion
  133.0 0.0 copy-done.1
  133.0 37.3 %all_to_all.27 = bf16[32,4,64,128]{3,2,1,0:T(8,128)(2,1)} all-to-all(bf16[32,4,64,128]{3,2,1,0:T(8,128)(2,1)} %bitcast.84), channel_id=1, replica_groups=mesh['sub'=32,'rep'=4] {'sub'}, dimensions={0} | all-to-all | bytes 4194304 | tf_op jit(solution)/shard_map/all_to_all | solution.py:87
  170.3 3.3 %gather_fusion.1 = bf16[64,64,128]{2,1,0:T(8,128)(2,1)} fusion(bf16[32,4,64,128]{3,2,1,0:T(8,128)(2,1)} %all_to_all.27, s32[64]{0:T(128)S(1)} %bitcast.88), kind=kCustom, calls=%fused_computation.1 | custom fusion | bytes 2097664 | tf_op jit(solution)/shard_map/gather | solution.py:88
  173.6 9.1 %fusion.1 = bf16[8,8,8,8,128]{4,3,2,1,0:T(8,128)(2,1)S(1)} fusion(bf16[8,1024,1024]{2,1,0:T(8,128)(2,1)} %param.8, bf16[8,8,8,8,128]{4,3,2,1,0:T(8,128)(2,1)} %bitcast.87), kind=kOutput, calls=%fused_computation.12 | convolution fusion | flops 1074266112 | bytes 18874368 | tf_op jit(solution)/shard_map/skl,slm->skm/dot_general | solution.py:19
  182.7 1.3 copy.62
  184.0 1.9 broadcast.81
  185.8 9.8 %scatter_fusion.3 = bf16[32,4,64,128]{3,2,1,0:T(8,128)(2,1)} fusion(bf16[32,4,64,128]{3,2,1,0:T(8,128)(2,1)} %broadcast.81, s32[64]{0:T(128)S(1)} %get-tuple-element.2, bf16[64,64,128]{2,1,0:T(8,128)(2,1)} %bitcast.85), kind=kCustom, calls=%fused_computation.5 | custom fusion | bytes 3146240 | tf_op jit(solution)/shard_map/scatter | solution.py:45
  195.7 32.1 %all_to_all.28 = bf16[32,4,64,128]{3,2,1,0:T(8,128)(2,1)S(1)} all-to-all(bf16[32,4,64,128]{3,2,1,0:T(8,128)(2,1)} %scatter_fusion.3), channel_id=1, replica_groups=mesh['sub'=32,'rep'=4] {'sub'}, dimensions={0} | all-to-all | bytes 4194304 | tf_op jit(solution)/shard_map/all_to_all | solution.py:91
  227.7 2.5 %bitcast_convert_fusion = f32[128,64,128]{2,1,0:T(8,128)} fusion(bf16[32,4,64,128]{3,2,1,0:T(8,128)(2,1)S(1)} %all_to_all.28), kind=kLoop, calls=%fused_computation.7 | loop fusion | flops 1048576 | bytes 6291456 | tf_op jit(solution)/shard_map/convert_element_type | solution.py:50
  230.3 13.5 %scatter_fusion.4 = f32[16,64,128]{2,1,0:T(8,128)S(1)} fusion(f32[16,64,128]{2,1,0:T(8,128)S(1)} %broadcast.74, s32[128]{0:T(128)S(1)} %fusion.12, f32[128,64,128]{2,1,0:T(8,128)} %bitcast_convert_fusion), kind=kCustom, calls=%fused_computation.6 | custom fusion | flops 1048576 | bytes 12583424 | tf_op jit(solution)/shard_map/scatter-add | solution.py:51
  243.9 0.9 fusion.5
  (13 shorter events, 0.3 us)
Async XLA Ops:
  0.6 126.1 %copy-start = (bf16[1024,1024]{1,0:T(8,128)(2,1)S(1)}, bf16[1024,1024]{1,0:T(8,128)(2,1)}, u32[]{:S(2)}) copy-start(bf16[1024,1024]{1,0:T(8,128)(2,1)} %param.13) | copy-start | bytes 6291460
  8.8 30.7 %all-to-all-start = ((s32[32,1,4]{2,1,0:T(1,128)}), s32[32,1,4]{2,1,0:T(1,128)S(1)}, u32[]{:S(2)}, u32[]{:S(2)}) async-start(s32[32,1,4]{2,1,0:T(1,128)} %copy.33), calls=%async_computation | async-start | bytes 32768 | tf_op jit(solution)/shard_map/all_to_all | solution.py:73
  39.5 7.6 %copy-start.2 = (s32[2048]{0:T(1024)S(1)}, s32[2048]{0:T(1024)}, u32[]{:S(2)}) copy-start(s32[2048]{0:T(1024)} %param.11) | copy-start | bytes 24580
  39.5 35.9 %all-to-all-start.1 = ((bf16[32,4,64,128]{3,2,1,0:T(8,128)(2,1)}), bf16[32,4,64,128]{3,2,1,0:T(8,128)(2,1)}, u32[]{:S(2)}, u32[]{:S(2)}) async-start(bf16[32,4,64,128]{3,2,1,0:T(8,128)(2,1)} %scatter_fusion.1), calls=%async_computation.1 | async-start | bytes 4194304 | tf_op jit(solution)/shard_map/all_to_all | solution.py:72
  96.0 2.1 collective-permute-start
  98.2 7.6 %collective-permute-start.1 = (f32[64,1024]{1,0:T(8,128)S(1)}, f32[64,1024]{1,0:T(8,128)S(1)}, u32[]{:S(2)}, u32[]{:S(2)}) collective-permute-start(f32[64,1024]{1,0:T(8,128)S(1)} %add.70), channel_id=1, source_target_pairs={{0,8},{4,12},{8,0},{12,4},{16,24},{20,28},{24,16},{28,20},{32,40},... | collective-permute-start | bytes 786440 | tf_op jit(solution)/shard_map/ppermute | solution.py:13
  105.8 8.2 %collective-permute-start.2 = (f32[64,1024]{1,0:T(8,128)S(1)}, f32[64,1024]{1,0:T(8,128)S(1)}, u32[]{:S(2)}, u32[]{:S(2)}) collective-permute-start(f32[64,1024]{1,0:T(8,128)S(1)} %add.71), channel_id=1, source_target_pairs={{0,16},{4,20},{8,24},{12,28},{16,0},{20,4},{24,8},{28,12},{32,48},... | collective-permute-start | bytes 786440 | tf_op jit(solution)/shard_map/ppermute | solution.py:13
  114.0 5.8 %collective-permute-start.3 = (f32[64,1024]{1,0:T(8,128)S(1)}, f32[64,1024]{1,0:T(8,128)S(1)}, u32[]{:S(2)}, u32[]{:S(2)}) collective-permute-start(f32[64,1024]{1,0:T(8,128)S(1)} %add.72), channel_id=1, source_target_pairs={{0,32},{4,36},{8,40},{12,44},{16,48},{20,52},{24,56},{28,60},{32,0... | collective-permute-start | bytes 786440 | tf_op jit(solution)/shard_map/ppermute | solution.py:13
  119.8 6.9 %collective-permute-start.4 = (f32[64,1024]{1,0:T(8,128)S(1)}, f32[64,1024]{1,0:T(8,128)}, u32[]{:S(2)}, u32[]{:S(2)}) collective-permute-start(f32[64,1024]{1,0:T(8,128)S(1)} %add.73), channel_id=1, source_target_pairs={{0,64},{4,68},{8,72},{12,76},{16,80},{20,84},{24,88},{28,92},{32,9... | collective-permute-start | bytes 786440 | tf_op jit(solution)/shard_map/ppermute | solution.py:13
  130.8 2.2 copy-start.1
